TPU v7x, 32 devices: a whole 2x2x4 slice. The times are simulated.
32 devices in a mesh: src: 16 (over z, x, core), tgt: 2 (over y).
Axes of the slice: x: 2, y: 2, z: 4, core: 2. Of those that a mesh axis runs over, the one named last changes fastest.
Arguments:
- source_embed: bfloat16 [128, 65536], P(None, 'src'), may hold values from -1 to 1
- target_embed: bfloat16 [128, 1024], P(None, 'tgt'), may hold values from -1 to 1
- source_expr: bfloat16 [128, 65536], P(None, 'src'), may hold values from -0.5390625 to 0.5390625
- target_expr: bfloat16 [128, 1024], P(None, 'tgt'), may hold values from -0.5390625 to 0.5390625
- current_plan: bfloat16 [65536, 1024], P('src', 'tgt'), as said below
- source_mass: float32 [65536], P('src'), may hold values from 0.25 to 4
- target_mass: float32 [1024], P('tgt'), may hold values from 0.25 to 4
- source_potential: float32 [65536], P('src'), may hold values from -16 to 16
- target_genes: bfloat16 [1024, 256], P('tgt'), may hold values from -6 to 6
Outputs:
- imputed: bfloat16 [65536, 256], P(('src', 'tgt'))
Inputs may be any that keep to these rules, and one draw needn't show every extreme that they name: Every entry of current_plan is positive.
All inputs are finite; a program needn't handle non-finite values.
Results may differ from a plain program's by a relative error of at most 0.014.
Values may be sent and summed in bfloat16 or wider, within the bound.
A program may use at most 64 MiB of HBM per device.

v0:
```python
import jax
import jax.numpy as jnp
from jax import lax
from jax.sharding import PartitionSpec as P

ITERS = 2
epsilon = 0.05
geometry_weight = 4.0


def joined(value, axis, join):
    pieces = jax.tree.map(lambda part: lax.all_gather(part, axis), value)
    head = jax.tree.map(lambda part: part[0], pieces)
    tail = jax.tree.map(lambda part: part[1:], pieces)
    so_far, _ = lax.scan(lambda so_far, piece: (join(so_far, piece), None), head, tail)
    return so_far


def factors(embed):
    widened = embed.astype(jnp.float32)
    squares = jnp.sum(widened * widened, axis=0)
    unit_row = jnp.ones_like(squares)
    left_factor = jnp.concatenate([squares[None, :], unit_row[None, :], -2.0 * widened], axis=0)
    right_factor = jnp.concatenate([unit_row[None, :], squares[None, :], widened], axis=0)
    return (left_factor, right_factor)


def combine_pair(earlier, later):
    maximum = jnp.maximum(earlier[0], later[0])
    return (
        maximum,
        earlier[1] * jnp.exp(earlier[0] - maximum) + later[1] * jnp.exp(later[0] - maximum),
    )


def column_logsum(scores):
    local_max = jnp.max(scores, axis=0)
    local_sum = jnp.sum(jnp.exp(scores - local_max[None, :]), axis=0)
    maximum, totals = joined((local_max, local_sum), "src", combine_pair)
    return maximum + jnp.log(totals)


def row_logsum(scores):
    local_max = jnp.max(scores, axis=1)
    local_sum = jnp.sum(jnp.exp(scores - local_max[:, None]), axis=1)
    maximum, totals = joined((local_max, local_sum), "tgt", combine_pair)
    return maximum + jnp.log(totals)


def shards(
    source_embed,
    target_embed,
    source_expr,
    target_expr,
    current_plan,
    source_mass,
    target_mass,
    source_potential,
    target_genes,
):
    highest = lax.Precision.HIGHEST
    spot_rows = source_embed.shape[1]
    spot_cols = target_embed.shape[1]
    total_pairs = float(spot_rows * lax.axis_size("src") * spot_cols * lax.axis_size("tgt"))
    left_src, right_src = factors(source_embed)
    left_tgt, right_tgt = factors(target_embed)
    projected = jnp.dot(
        current_plan.astype(jnp.float32),
        right_tgt.T,
        precision=highest,
        preferred_element_type=jnp.float32,
    )
    partial_core = jnp.dot(
        right_src, projected, precision=highest, preferred_element_type=jnp.float32
    )
    core_matrix = lax.psum(partial_core, ("src", "tgt")) / total_pairs
    geometry_right = jnp.dot(
        core_matrix, left_tgt, precision=highest, preferred_element_type=jnp.float32
    )
    geometry = lax.dot_general(
        left_src,
        geometry_right,
        (((0,), (0,)), ((), ())),
        precision=highest,
        preferred_element_type=jnp.float32,
    )
    feature = lax.dot_general(
        source_expr, target_expr, (((0,), (0,)), ((), ())), preferred_element_type=jnp.float32
    )
    cost_tile = -2.0 * (feature + geometry_weight * geometry)
    log_src = jnp.log(source_mass)
    log_tgt = jnp.log(target_mass)
    potential_src = source_potential
    potential_tgt = jnp.zeros((spot_cols,), jnp.float32)
    for iteration in range(ITERS):
        potential_tgt = epsilon * log_tgt - epsilon * column_logsum(
            (potential_src[:, None] - cost_tile) / epsilon
        )
        potential_src = epsilon * log_src - epsilon * row_logsum(
            (potential_tgt[None, :] - cost_tile) / epsilon
        )
    weights = jnp.exp(
        (potential_src[:, None] + potential_tgt[None, :] - cost_tile) / epsilon
    ).astype(jnp.bfloat16)
    row_share = spot_rows // lax.axis_size("tgt")
    row_offset = lax.axis_index("tgt") * row_share
    mass_rows = lax.dynamic_slice_in_dim(source_mass, row_offset, row_share)
    numerator = lax.psum_scatter(
        jnp.dot(weights, target_genes, preferred_element_type=jnp.float32).astype(jnp.bfloat16),
        "tgt",
        scatter_dimension=0,
        tiled=True,
    ).astype(jnp.float32)
    return (numerator / mass_rows[:, None]).astype(jnp.bfloat16)


def solution(mesh):
    return jax.shard_map(
        shards,
        mesh=mesh,
        in_specs=(
            P(None, "src"),
            P(None, "tgt"),
            P(None, "src"),
            P(None, "tgt"),
            P("src", "tgt"),
            P("src"),
            P("tgt"),
            P("src"),
            P("tgt", None),
        ),
        out_specs=P(("src", "tgt"), None),
        check_vma=False,
    )
```

profile of v0, /device:TPU:0, one launch (start us, length us, event | category | flops | bytes accessed | tf_op | source)
XLA Modules:
  0.0 319.4 jit_solution(5949856165096476949)
XLA Ops:
  6.5 0.0 copy-start
  6.5 0.0 all-reduce.2.cloned.1.call-start
  6.5 0.0 copy-start.3
  6.5 1.1 multiply_reduce_fusion.1
  7.7 1.2 convert_element_type.20
  8.9 1.6 broadcast_multiply_fusion
  10.4 1.4 convert_element_type.19
  11.9 0.0 copy-done.3
  11.9 4.3 %fusion.18 = f32[130,4096]{1,0:T(8,128)S(1)} fusion(bf16[4096,512]{1,0:T(8,128)(2,1)S(1)} %copy-done.3, f32[128,512]{1,0:T(8,128)S(1)} %convert_element_type.20, f32[1,512]{1,0:T(1,128)S(1)} %bitcast.56, f32[1,512]{1,0:T(1,128)S(1)} %broadcast.34), kind=kOutput, calls=%fused_computation.38 | convolution fusion | flops 3271690240 | bytes 6590464 | tf_op jit(solution)/shard_map/dot_general | solution.py:67
  16.2 2.8 fusion.12
  19.0 0.0 copy-start.5
  19.0 0.0 all-reduce.2.cloned.1.call-update
  19.0 0.2 reduce-scatter.2.cloned.1.call-start
  19.3 0.0 copy-done
  19.3 5.4 %fusion.50 = f32[4096,512]{1,0:T(8,128)} fusion(bf16[128,4096]{1,0:T(8,128)(2,1)S(1)} %copy-done, bf16[128,512]{1,0:T(8,128)(2,1)} %param.16), kind=kOutput, calls=%fused_computation.86 | convolution fusion | flops 536870912 | bytes 9568256 | tf_op jit(solution)/shard_map/dot_general | solution.py:87
  24.7 117.4 %all-reduce.2.cloned.1.call-done = f32[130,130]{1,0:T(8,128)} async-done(((f32[130,130]{1,0:T(8,128)}), f32[130,130]{1,0:T(8,128)}) %all-reduce.2.cloned.1.call-update) | async-done | bytes 67616 | tf_op jit(solution)/shard_map/psum | solution.py:76
  142.1 1.3 fusion.24
  143.4 0.0 copy-done.5
  143.4 11.4 %fusion = (f32[512]{0:T(512)S(1)}, f32[4096,512]{1,0:T(8,128)S(1)}) fusion(f32[4096]{0:T(1024)S(1)} %copy-done.5, f32[4096,512]{1,0:T(8,128)} %fusion.50, f32[130,512]{1,0:T(8,128)S(1)} %fusion.24, f32[128,4096]{1,0:T(8,128)S(1)} %get-tuple-element.123, f32[1,4096]{1,0:T(1,128)S(1)} %broadcast.33, f32[1,4096]{1,0:T(1,128)S(1)} %bitcast.47), kind=kOutput, calls=%fused_computation.16 | convolution fusion | flops 3285204480 | bytes 19191808 | tf_op jit(solution)/shard_map/dot_general | solution.py:80
  154.8 0.0 copy-start.1
  154.8 0.0 copy-start.6
  154.8 3.2 %copy-done.1 = f32[4096,512]{1,0:T(8,128)} copy-done((f32[4096,512]{1,0:T(8,128)}, f32[4096,512]{1,0:T(8,128)S(1)}, u32[]{:S(2)}) %copy-start.1) | copy-done | bytes 8388632
  158.0 1.8 exponential_reduce_fusion.3
  159.8 22.9 %all-gather.9 = f32[16,1,512]{2,1,0:T(1,128)S(1)} all-gather(f32[1,1,512]{2,1,0:T(1,128)S(1)} %bitcast.61), channel_id=3, replica_groups=mesh['src'=16,'tgt'=2] {'src'}, dimensions={0}, use_global_device_ids=true | all-gather | bytes 34816 | tf_op jit(solution)/shard_map/all_gather | solution.py:12
  182.7 17.5 %all-gather.8 = f32[16,1,512]{2,1,0:T(1,128)S(1)} all-gather(f32[1,1,512]{2,1,0:T(1,128)S(1)} %bitcast.58), channel_id=2, replica_groups=mesh['src'=16,'tgt'=2] {'src'}, dimensions={0}, use_global_device_ids=true | all-gather | bytes 34816 | tf_op jit(solution)/shard_map/all_gather | solution.py:12
  200.2 0.8 while.4
  201.0 0.0 copy-start.2
  201.0 0.0 copy-done.6
  201.0 0.0 copy-start.4
  201.1 4.4 %fusion.1 = f32[4096]{0:T(1024)S(1)} fusion(f32[4096,512]{1,0:T(8,128)} %copy-done.1, f32[512]{0:T(512)S(1)} %multiply_subtract_fusion.1), kind=kLoop, calls=%fused_computation.17 | loop fusion | flops 6287360 | bytes 8407040 | tf_op jit(solution)/shard_map/reduce_max | solution.py:44
  205.5 1.3 copy-done.2
  206.8 2.2 exponential_reduce_fusion.2
  209.0 4.4 %all-gather.2 = f32[8192]{0:T(1024)S(1)} all-gather(f32[4096]{0:T(1024)S(1)} %fusion.1), channel_id=4, replica_groups=mesh['src'=16,'tgt'=2] {'tgt'}, dimensions={0}, use_global_device_ids=true | all-gather | bytes 49152 | tf_op jit(solution)/shard_map/all_gather | solution.py:12
  213.4 4.4 %all-gather.3 = f32[8192]{0:T(1024)S(1)} all-gather(f32[4096]{0:T(1024)S(1)} %exponential_reduce_fusion.2), channel_id=5, replica_groups=mesh['src'=16,'tgt'=2] {'tgt'}, dimensions={0}, use_global_device_ids=true | all-gather | bytes 49152 | tf_op jit(solution)/shard_map/all_gather | solution.py:12
  217.8 0.0 copy-done.4
  217.8 1.0 fusion.2
  218.8 1.8 exponential_reduce_fusion.1
  220.6 18.9 %all-gather.11 = f32[16,1,512]{2,1,0:T(1,128)S(1)} all-gather(f32[1,1,512]{2,1,0:T(1,128)S(1)} %bitcast.60), channel_id=7, replica_groups=mesh['src'=16,'tgt'=2] {'src'}, dimensions={0}, use_global_device_ids=true | all-gather | bytes 34816 | tf_op jit(solution)/shard_map/all_gather | solution.py:12
  239.5 17.7 %all-gather.10 = f32[16,1,512]{2,1,0:T(1,128)S(1)} all-gather(f32[1,1,512]{2,1,0:T(1,128)S(1)} %bitcast.59), channel_id=6, replica_groups=mesh['src'=16,'tgt'=2] {'src'}, dimensions={0}, use_global_device_ids=true | all-gather | bytes 34816 | tf_op jit(solution)/shard_map/all_gather | solution.py:12
  257.2 0.8 while.5
  258.1 0.0 slice-start
  258.1 0.0 copy-start.7
  258.1 4.4 %fusion.3 = f32[4096]{0:T(1024)S(1)} fusion(f32[4096,512]{1,0:T(8,128)} %copy-done.1, f32[512]{0:T(512)S(1)} %multiply_subtract_fusion), kind=kLoop, calls=%fused_computation.19 | loop fusion | flops 6287360 | bytes 8407040 | tf_op jit(solution)/shard_map/reduce_max | solution.py:44
  262.5 0.0 slice-start.1
  262.5 5.1 %exponential_reduce_fusion = f32[4096]{0:T(1024)S(1)} fusion(f32[4096,512]{1,0:T(8,128)} %copy-done.1, f32[4096]{0:T(1024)S(1)} %fusion.3, f32[512]{0:T(512)S(1)} %multiply_subtract_fusion), kind=kLoop, calls=%fused_computation.7 | loop fusion | flops 8384512 | bytes 8423424 | tf_op jit(solution)/shard_map/reduce_sum | solution.py:45
  267.6 4.4 %all-gather.6 = f32[8192]{0:T(1024)S(1)} all-gather(f32[4096]{0:T(1024)S(1)} %fusion.3), channel_id=8, replica_groups=mesh['src'=16,'tgt'=2] {'tgt'}, dimensions={0}, use_global_device_ids=true | all-gather | bytes 49152 | tf_op jit(solution)/shard_map/all_gather | solution.py:12
  272.0 4.4 %all-gather.7 = f32[8192]{0:T(1024)S(1)} all-gather(f32[4096]{0:T(1024)S(1)} %exponential_reduce_fusion), channel_id=9, replica_groups=mesh['src'=16,'tgt'=2] {'tgt'}, dimensions={0}, use_global_device_ids=true | all-gather | bytes 49152 | tf_op jit(solution)/shard_map/all_gather | solution.py:12
  276.5 0.0 slice-done
  276.5 0.0 copy-done.7
  276.5 0.0 slice-done.1
  276.5 3.2 %convolution_convert_fusion = bf16[4096,256]{1,0:T(8,128)(2,1)} fusion(bf16[512,256]{1,0:T(8,128)(2,1)S(1)} %copy-done.7, f32[4096,512]{1,0:T(8,128)S(1)} %bitcast.41, f32[4096]{0:T(1024)S(1)} %fusion.36, f32[512]{0:T(512)S(1)} %multiply_subtract_fusion), kind=kOutput, calls=%fused_computation.20 | convolution fusion | flops 1083179008 | bytes 10766336 | tf_op jit(solution)/shard_map/dot_general | solution.py:109
  279.7 0.0 reduce-scatter.2.cloned.1.call-update
  279.8 30.3 %reduce-scatter.2.cloned.1.call-done = bf16[2048,256]{1,0:T(8,128)(2,1)} async-done(((bf16[4096,256]{1,0:T(8,128)(2,1)}), bf16[2048,256]{1,0:T(8,128)(2,1)}) %reduce-scatter.2.cloned.1.call-update) | async-done | bytes 1048592 | tf_op jit(solution)/shard_map/reduce_scatter | solution.py:108
  310.1 2.5 divide_convert_fusion
  (80 shorter events, 1.1 us)
Async XLA Ops:
  6.5 12.7 %copy-start = (bf16[128,4096]{1,0:T(8,128)(2,1)S(1)}, bf16[128,4096]{1,0:T(8,128)(2,1)}, u32[]{:S(2)}) copy-start(bf16[128,4096]{1,0:T(8,128)(2,1)} %param.15) | copy-start | bytes 3145732
  6.5 135.5 %all-reduce.2.cloned.1.call-start = ((), (), s32[]{:S(2)}) async-start(), calls=%async_computation.1 | async-start | bytes 278528 | tf_op jit(solution)/shard_map/psum | solution.py:76
  6.5 5.4 %copy-start.3 = (bf16[4096,512]{1,0:T(8,128)(2,1)S(1)}, bf16[4096,512]{1,0:T(8,128)(2,1)}, u32[]{:S(2)}) copy-start(bf16[4096,512]{1,0:T(8,128)(2,1)} %param.17) | copy-start | bytes 12582916
  19.0 124.4 %copy-start.5 = (f32[4096]{0:T(1024)S(1)}, f32[4096]{0:T(1024)}, u32[]{:S(2)}) copy-start(f32[4096]{0:T(1024)} %param.20) | copy-start | bytes 49156
  19.0 291.0 %reduce-scatter.2.cloned.1.call-start = ((), (), s32[]{:S(2)}) async-start(), calls=%async_computation.2 | async-start | bytes 3145728 | tf_op jit(solution)/shard_map/reduce_scatter | solution.py:108
  154.8 3.2 %copy-start.1 = (f32[4096,512]{1,0:T(8,128)}, f32[4096,512]{1,0:T(8,128)S(1)}, u32[]{:S(2)}) copy-start(f32[4096,512]{1,0:T(8,128)S(1)} %get-tuple-element.128) | copy-start | bytes 25165828
  154.8 46.2 %copy-start.6 = (f32[512]{0:T(512)S(1)}, f32[512]{0:T(512)}, u32[]{:S(2)}) copy-start(f32[512]{0:T(512)} %param.19) | copy-start | bytes 6148
  201.0 5.8 %copy-start.2 = (f32[4096,512]{1,0:T(8,128)S(1)}, f32[4096,512]{1,0:T(8,128)}, u32[]{:S(2)}) copy-start(f32[4096,512]{1,0:T(8,128)} %copy-done.1) | copy-start | bytes 25165828
  201.0 16.8 %copy-start.4 = (f32[4096]{0:T(1024)S(1)}, f32[4096]{0:T(1024)}, u32[]{:S(2)}) copy-start(f32[4096]{0:T(1024)} %param.18) | copy-start | bytes 49156
  258.1 18.4 %slice-start = ((s8[8388608]{0:T(1024)(128)(4,1)}), s8[4194304]{0:T(1024)(128)(4,1)S(1)}, s32[]{:S(2)}) async-start(s8[8388608]{0:T(1024)(128)(4,1)} %bitcast.40), calls=%async_computation.3 | async-start | bytes 8388608
  258.1 18.4 %copy-start.7 = (bf16[512,256]{1,0:T(8,128)(2,1)S(1)}, bf16[512,256]{1,0:T(8,128)(2,1)}, u32[]{:S(2)}) copy-start(bf16[512,256]{1,0:T(8,128)(2,1)} %param.21) | copy-start | bytes 786436
  262.5 14.0 %slice-start.1 = ((s8[8388608]{0:T(1024)(128)(4,1)}), s8[4194304]{0:T(1024)(128)(4,1)S(1)}, s32[]{:S(2)}) async-start(s8[8388608]{0:T(1024)(128)(4,1)} %bitcast.40), calls=%async_computation.4 | async-start | bytes 8388608
Sparse Core Ops, SparseCore 0:
  19.1 122.8 all-reduce.1
  279.9 30.1 reduce-scatter.1
where the time goes:
time: 320 us; the launch traced here: 319 us
  waiting for transfers between devices  148 us (46%)
  blocking collectives  94.5 us (30%)
  other arithmetic  29.3 us (9%)
  matrix products  28.4 us (9%)
  between operations  13.7 us (4%)
  local copies, waits for them, and re-layouts  4.93 us (2%)
    psum x1, waiting for transfers between devices, shards(): core_matrix = lax.psum(partial_core, ('src', 'tgt')) / total_pairs  117 us
    all_gather x8, blocking collectives, joined(): pieces = jax.tree.map(lambda part: lax.all_gather(part, axis), value)  94.5 us
    reduce_scatter x1, waiting for transfers between devices, shards(): lax.psum_scatter(jnp.dot(weights, target_genes, preferred_element_type=jn...  30.3 us
    dot_general x1, matrix products, shards(): lax.dot_general(left_src, geometry_right, (((0,), (0,)), ((), ())), preci...  11.4 us
    reduce_max x2, other arithmetic, row_logsum(): local_max = jnp.max(scores, axis=1)  8.87 us
    reduce_sum x2, other arithmetic, row_logsum(): local_sum = jnp.sum(jnp.exp(scores - local_max[:, None]), axis=1)  7.28 us
  transfers between devices with their start and end apart: 2, of which 2 were waited for; matrix products, arithmetic and copies ran while one was open for 2% of the time, Pallas kernels for 0%

commit v1 on v0

--- a/solution.py
+++ b/solution.py
@@ -73,7 +73,7 @@
     partial_core = jnp.dot(
         right_src, projected, precision=highest, preferred_element_type=jnp.float32
     )
-    core_matrix = lax.psum(partial_core, ("src", "tgt")) / total_pairs
+    core_matrix = jnp.sum(lax.all_gather(partial_core, ("src", "tgt")), axis=0) / total_pairs
     geometry_right = jnp.dot(
         core_matrix, left_tgt, precision=highest, preferred_element_type=jnp.float32
     )

time: 320 us -> 261 us (0.82)
  waiting for transfers between devices: 148 us -> 90.6 us
    psum x1 -> x0, waiting for transfers between devices: 117 us -> none  [shards(): core_matrix = lax.psum(partial_core, ('src', 'tgt')) / total_pairs]
    all_gather x0 -> x1, waiting for transfers between devices: none -> 61.1 us  [shards(): lax.all_gather(partial_core, ('src', 'tgt'))]
where the time goes in v1:
time: 261 us
  blocking collectives  91.4 us (35%)
  waiting for transfers between devices  90.6 us (35%)
  other arithmetic  31.9 us (12%)
  matrix products  26.6 us (10%)
  between operations  13.7 us (5%)
  local copies, waits for them, and re-layouts  5.53 us (2%)
    all_gather x8, blocking collectives, joined(): pieces = jax.tree.map(lambda part: lax.all_gather(part, axis), value)  91.4 us
    all_gather x1, waiting for transfers between devices, shards(): lax.all_gather(partial_core, ('src', 'tgt'))  61.1 us
    reduce_scatter x1, waiting for transfers between devices, shards(): lax.psum_scatter(jnp.dot(weights, target_genes, preferred_element_type=jn...  29.5 us
    dot_general x1, matrix products, shards(): lax.dot_general(left_src, geometry_right, (((0,), (0,)), ((), ())), preci...  11.4 us
    reduce_max x2, other arithmetic, row_logsum(): local_max = jnp.max(scores, axis=1)  8.87 us
    reduce_sum x2, other arithmetic, row_logsum(): local_sum = jnp.sum(jnp.exp(scores - local_max[:, None]), axis=1)  7.28 us
  transfers between devices with their start and end apart: 2, of which 2 were waited for; matrix products, arithmetic and copies ran while one was open for 2% of the time, Pallas kernels for 0%

profile of v1, /device:TPU:0, one launch (start us, length us, event | category | flops | bytes accessed | tf_op | source)
XLA Modules:
  0.0 260.6 jit_solution(4137727268448381531)
XLA Ops:
  6.5 0.0 copy-start
  6.5 0.0 all-gather.16.cloned.1.call-start
  6.5 0.0 copy-start.3
  6.5 1.1 multiply_reduce_fusion.1
  7.7 1.2 convert_element_type.20
  8.9 0.0 copy-start.6
  8.9 1.6 broadcast_multiply_fusion
  10.5 0.0 copy-start.4
  10.5 1.4 convert_element_type.19
  12.0 0.0 copy-done.3
  12.0 4.3 %fusion.21 = f32[130,4096]{1,0:T(8,128)S(1)} fusion(bf16[4096,512]{1,0:T(8,128)(2,1)S(1)} %copy-done.3, f32[128,512]{1,0:T(8,128)S(1)} %convert_element_type.20, f32[1,512]{1,0:T(1,128)S(1)} %bitcast.58, f32[1,512]{1,0:T(1,128)S(1)} %broadcast.34), kind=kOutput, calls=%fused_computation.39 | convolution fusion | flops 3271690240 | bytes 6590464 | tf_op jit(solution)/shard_map/dot_general | solution.py:67
  16.3 0.0 copy-done.4
  16.3 0.0 copy-start.5
  16.3 0.6 copy-done.5
  16.9 2.8 %fusion.18 = f32[1,130,130]{2,1,0:T(8,128)} fusion(f32[130,4096]{1,0:T(8,128)S(1)} %fusion.21, f32[128,4096]{1,0:T(8,128)S(1)} %convert_element_type.19, f32[1,4096]{1,0:T(1,128)S(1)} %bitcast.48, f32[1,4096]{1,0:T(1,128)S(1)} %broadcast.33), kind=kOutput, calls=%fused_computation.37 | convolution fusion | flops 831733760 | bytes 4327440 | tf_op jit(solution)/shard_map/dot_general | solution.py:73
  19.7 0.0 all-gather.16.cloned.1.call-update
  19.7 0.2 reduce-scatter.2.cloned.1.call-start
  19.9 0.0 copy-done
  19.9 0.0 copy-done.6
  19.9 4.5 %fusion.53 = f32[4096,512]{1,0:T(8,128)} fusion(bf16[128,4096]{1,0:T(8,128)(2,1)S(1)} %copy-done, bf16[128,512]{1,0:T(8,128)(2,1)S(1)} %copy-done.6), kind=kOutput, calls=%fused_computation.87 | convolution fusion | flops 536870912 | bytes 9568256 | tf_op jit(solution)/shard_map/dot_general | solution.py:87
  24.4 61.1 %all-gather.16.cloned.1.call-done = f32[32,130,130]{2,1,0:T(8,128)} async-done(((f32[1,130,130]{2,1,0:T(8,128)}), f32[32,130,130]{2,1,0:T(8,128)}) %all-gather.16.cloned.1.call-update) | async-done | bytes 2163216 | tf_op jit(solution)/shard_map/all_gather | solution.py:76
  85.5 2.6 reduce_sum.65
  88.1 0.4 fusion.27
  88.5 0.0 copy-start.8
  88.5 11.4 %fusion = (f32[512]{0:T(512)S(1)}, f32[4096,512]{1,0:T(8,128)S(1)}) fusion(f32[4096]{0:T(1024)} %param.20, f32[4096,512]{1,0:T(8,128)} %fusion.53, f32[130,512]{1,0:T(8,128)S(1)} %fusion.27, f32[128,4096]{1,0:T(8,128)S(1)} %get-tuple-element.123, f32[1,4096]{1,0:T(1,128)} %copy-done.5, f32[1,4096]{1,0:T(1,128)} %bitcast.49), kind=kOutput, calls=%fused_computation.16 | convolution fusion | flops 3285204480 | bytes 19191808 | tf_op jit(solution)/shard_map/dot_general | solution.py:80
  100.0 0.0 copy-start.1
  100.0 0.0 copy-start.9
  100.0 3.2 %copy-done.1 = f32[4096,512]{1,0:T(8,128)} copy-done((f32[4096,512]{1,0:T(8,128)}, f32[4096,512]{1,0:T(8,128)S(1)}, u32[]{:S(2)}) %copy-start.1) | copy-done | bytes 8388632
  103.2 0.0 copy-done.8
  103.2 1.8 exponential_reduce_fusion.3
  105.0 19.7 %all-gather.11 = f32[16,1,512]{2,1,0:T(1,128)S(1)} all-gather(f32[1,1,512]{2,1,0:T(1,128)S(1)} %bitcast.63), channel_id=4, replica_groups=mesh['src'=16,'tgt'=2] {'src'}, dimensions={0}, use_global_device_ids=true | all-gather | bytes 34816 | tf_op jit(solution)/shard_map/all_gather | solution.py:12
  124.7 17.5 %all-gather.10 = f32[16,1,512]{2,1,0:T(1,128)S(1)} all-gather(f32[1,1,512]{2,1,0:T(1,128)S(1)} %bitcast.60), channel_id=3, replica_groups=mesh['src'=16,'tgt'=2] {'src'}, dimensions={0}, use_global_device_ids=true | all-gather | bytes 34816 | tf_op jit(solution)/shard_map/all_gather | solution.py:12
  142.2 0.8 while.4
  143.0 0.0 copy-start.2
  143.1 0.0 copy-done.9
  143.1 0.0 copy-start.7
  143.1 4.4 %fusion.1 = f32[4096]{0:T(1024)S(1)} fusion(f32[4096,512]{1,0:T(8,128)} %copy-done.1, f32[512]{0:T(512)S(1)} %multiply_subtract_fusion.1), kind=kLoop, calls=%fused_computation.17 | loop fusion | flops 6287360 | bytes 8407040 | tf_op jit(solution)/shard_map/reduce_max | solution.py:44
  147.5 1.3 copy-done.2
  148.8 2.2 exponential_reduce_fusion.2
  151.0 4.4 %all-gather.3 = f32[8192]{0:T(1024)S(1)} all-gather(f32[4096]{0:T(1024)S(1)} %fusion.1), channel_id=5, replica_groups=mesh['src'=16,'tgt'=2] {'tgt'}, dimensions={0}, use_global_device_ids=true | all-gather | bytes 49152 | tf_op jit(solution)/shard_map/all_gather | solution.py:12
  155.4 4.4 %all-gather.4 = f32[8192]{0:T(1024)S(1)} all-gather(f32[4096]{0:T(1024)S(1)} %exponential_reduce_fusion.2), channel_id=6, replica_groups=mesh['src'=16,'tgt'=2] {'tgt'}, dimensions={0}, use_global_device_ids=true | all-gather | bytes 49152 | tf_op jit(solution)/shard_map/all_gather | solution.py:12
  159.8 0.0 copy-done.7
  159.9 1.0 fusion.2
  160.8 1.8 exponential_reduce_fusion.1
  162.7 18.9 %all-gather.13 = f32[16,1,512]{2,1,0:T(1,128)S(1)} all-gather(f32[1,1,512]{2,1,0:T(1,128)S(1)} %bitcast.62), channel_id=8, replica_groups=mesh['src'=16,'tgt'=2] {'src'}, dimensions={0}, use_global_device_ids=true | all-gather | bytes 34816 | tf_op jit(solution)/shard_map/all_gather | solution.py:12
  181.5 17.7 %all-gather.12 = f32[16,1,512]{2,1,0:T(1,128)S(1)} all-gather(f32[1,1,512]{2,1,0:T(1,128)S(1)} %bitcast.61), channel_id=7, replica_groups=mesh['src'=16,'tgt'=2] {'src'}, dimensions={0}, use_global_device_ids=true | all-gather | bytes 34816 | tf_op jit(solution)/shard_map/all_gather | solution.py:12
  199.3 0.8 while.5
  200.1 0.0 slice-start
  200.1 0.0 copy-start.10
  200.1 4.4 %fusion.3 = f32[4096]{0:T(1024)S(1)} fusion(f32[4096,512]{1,0:T(8,128)} %copy-done.1, f32[512]{0:T(512)S(1)} %multiply_subtract_fusion), kind=kLoop, calls=%fused_computation.19 | loop fusion | flops 6287360 | bytes 8407040 | tf_op jit(solution)/shard_map/reduce_max | solution.py:44
  204.5 0.0 slice-start.1
  204.6 5.1 %exponential_reduce_fusion = f32[4096]{0:T(1024)S(1)} fusion(f32[4096,512]{1,0:T(8,128)} %copy-done.1, f32[4096]{0:T(1024)S(1)} %fusion.3, f32[512]{0:T(512)S(1)} %multiply_subtract_fusion), kind=kLoop, calls=%fused_computation.7 | loop fusion | flops 8384512 | bytes 8423424 | tf_op jit(solution)/shard_map/reduce_sum | solution.py:45
  209.7 4.4 %all-gather.7 = f32[8192]{0:T(1024)S(1)} all-gather(f32[4096]{0:T(1024)S(1)} %fusion.3), channel_id=9, replica_groups=mesh['src'=16,'tgt'=2] {'tgt'}, dimensions={0}, use_global_device_ids=true | all-gather | bytes 49152 | tf_op jit(solution)/shard_map/all_gather | solution.py:12
  214.1 4.4 %all-gather.8 = f32[8192]{0:T(1024)S(1)} all-gather(f32[4096]{0:T(1024)S(1)} %exponential_reduce_fusion), channel_id=10, replica_groups=mesh['src'=16,'tgt'=2] {'tgt'}, dimensions={0}, use_global_device_ids=true | all-gather | bytes 49152 | tf_op jit(solution)/shard_map/all_gather | solution.py:12
  218.5 0.0 slice-done
  218.5 0.0 copy-done.10
  218.5 0.0 slice-done.1
  218.5 3.2 %convolution_convert_fusion = bf16[4096,256]{1,0:T(8,128)(2,1)} fusion(bf16[512,256]{1,0:T(8,128)(2,1)S(1)} %copy-done.10, f32[4096,512]{1,0:T(8,128)S(1)} %bitcast.43, f32[4096]{0:T(1024)S(1)} %fusion.39, f32[512]{0:T(512)S(1)} %multiply_subtract_fusion), kind=kOutput, calls=%fused_computation.20 | convolution fusion | flops 1083179008 | bytes 10766336 | tf_op jit(solution)/shard_map/dot_general | solution.py:109
  221.8 0.0 reduce-scatter.2.cloned.1.call-update
  221.8 29.5 %reduce-scatter.2.cloned.1.call-done = bf16[2048,256]{1,0:T(8,128)(2,1)} async-done(((bf16[4096,256]{1,0:T(8,128)(2,1)}), bf16[2048,256]{1,0:T(8,128)(2,1)}) %reduce-scatter.2.cloned.1.call-update) | async-done | bytes 1048592 | tf_op jit(solution)/shard_map/reduce_scatter | solution.py:108
  251.3 2.5 divide_convert_fusion
  (80 shorter events, 1.1 us)
Async XLA Ops:
  6.5 13.4 %copy-start = (bf16[128,4096]{1,0:T(8,128)(2,1)S(1)}, bf16[128,4096]{1,0:T(8,128)(2,1)}, u32[]{:S(2)}) copy-start(bf16[128,4096]{1,0:T(8,128)(2,1)} %param.15) | copy-start | bytes 3145732
  6.5 79.0 %all-gather.16.cloned.1.call-start = ((), (), s32[]{:S(2)}) async-start(), calls=%async_computation.2 | async-start | bytes 4595712 | tf_op jit(solution)/shard_map/all_gather | solution.py:76
  6.5 5.4 %copy-start.3 = (bf16[4096,512]{1,0:T(8,128)(2,1)S(1)}, bf16[4096,512]{1,0:T(8,128)(2,1)}, u32[]{:S(2)}) copy-start(bf16[4096,512]{1,0:T(8,128)(2,1)} %param.17) | copy-start | bytes 12582916
  8.9 11.0 %copy-start.6 = (bf16[128,512]{1,0:T(8,128)(2,1)S(1)}, bf16[128,512]{1,0:T(8,128)(2,1)}, u32[]{:S(2)}) copy-start(bf16[128,512]{1,0:T(8,128)(2,1)} %param.16) | copy-start | bytes 393220
  10.5 5.8 %copy-start.4 = (f32[4096]{0:T(1024)}, f32[4096]{0:T(1024)S(1)}, u32[]{:S(2)}) copy-start(f32[4096]{0:T(1024)S(1)} %get-tuple-element.124) | copy-start | bytes 49156
  16.3 0.6 copy-start.5
  19.7 231.6 %reduce-scatter.2.cloned.1.call-start = ((), (), s32[]{:S(2)}) async-start(), calls=%async_computation.1 | async-start | bytes 3145728 | tf_op jit(solution)/shard_map/reduce_scatter | solution.py:108
  88.5 14.7 %copy-start.8 = (f32[4096]{0:T(1024)S(1)}, f32[4096]{0:T(1024)}, u32[]{:S(2)}) copy-start(f32[4096]{0:T(1024)} %param.20) | copy-start | bytes 49156
  100.0 3.2 %copy-start.1 = (f32[4096,512]{1,0:T(8,128)}, f32[4096,512]{1,0:T(8,128)S(1)}, u32[]{:S(2)}) copy-start(f32[4096,512]{1,0:T(8,128)S(1)} %get-tuple-element.128) | copy-start | bytes 25165828
  100.0 43.1 %copy-start.9 = (f32[512]{0:T(512)S(1)}, f32[512]{0:T(512)}, u32[]{:S(2)}) copy-start(f32[512]{0:T(512)} %param.19) | copy-start | bytes 6148
  143.0 5.8 %copy-start.2 = (f32[4096,512]{1,0:T(8,128)S(1)}, f32[4096,512]{1,0:T(8,128)}, u32[]{:S(2)}) copy-start(f32[4096,512]{1,0:T(8,128)} %copy-done.1) | copy-start | bytes 25165828
  143.1 16.8 %copy-start.7 = (f32[4096]{0:T(1024)S(1)}, f32[4096]{0:T(1024)}, u32[]{:S(2)}) copy-start(f32[4096]{0:T(1024)} %param.18) | copy-start | bytes 49156
  200.1 18.4 %slice-start = ((s8[8388608]{0:T(1024)(128)(4,1)}), s8[4194304]{0:T(1024)(128)(4,1)S(1)}, s32[]{:S(2)}) async-start(s8[8388608]{0:T(1024)(128)(4,1)} %bitcast.42), calls=%async_computation.3 | async-start | bytes 8388608
  200.1 18.4 %copy-start.10 = (bf16[512,256]{1,0:T(8,128)(2,1)S(1)}, bf16[512,256]{1,0:T(8,128)(2,1)}, u32[]{:S(2)}) copy-start(bf16[512,256]{1,0:T(8,128)(2,1)} %param.21) | copy-start | bytes 786436
  204.5 14.0 %slice-start.1 = ((s8[8388608]{0:T(1024)(128)(4,1)}), s8[4194304]{0:T(1024)(128)(4,1)S(1)}, s32[]{:S(2)}) async-start(s8[8388608]{0:T(1024)(128)(4,1)} %bitcast.42), calls=%async_computation.4 | async-start | bytes 8388608
Sparse Core Ops, SparseCore 0:
  19.8 65.6 all-gather.15
  221.9 29.3 reduce-scatter.1
